TPU v7x, 128 devices: a whole 4x4x4 slice. The times are simulated.
128 devices in a mesh: gx: 8 (over y, core), gy: 4 (over z), gz: 4 (over x).
Axes of the slice: x: 4, y: 4, z: 4, core: 2. Of those that a mesh axis runs over, the one named last changes fastest.
Arguments:
- right_side: float32 [128, 64, 1024], P('gx', 'gy', 'gz'), may hold values from -8 to 8
- conductance: float32 [3, 128, 64, 1024], P(None, 'gx', 'gy', 'gz'), may hold values from 0.2 to 5
- storage: float32 [128, 64, 1024], P('gx', 'gy', 'gz'), may hold values from 0.05 to 0.8
- dirichlet: int32 [128, 64, 1024], P('gx', 'gy', 'gz'), may hold values 0 or 1
- basis: float32 [16, 128, 64, 1024], P(None, 'gx', 'gy', 'gz'), may hold values from -2 to 2
- coarse_inverse: float32 [2048, 2048], P(('gx', 'gy', 'gz')), may hold values from 0 to 2, as said below
Outputs:
- solution_field: float32 [128, 64, 1024], P('gx', 'gy', 'gz')
- residual: float32 [128, 64, 1024], P('gx', 'gy', 'gz')
Inputs may be any that keep to these rules, and one draw needn't show every extreme that they name: `coarse_inverse`: symmetric positive definite.
All inputs are finite; a program needn't handle non-finite values. No bound on the sum of `dirichlet` on one device may be relied on, other than what follows from the above.
Results may differ from a plain program's by a relative error of at most 0.0003.
Values sent between devices are 32-bit elements; how exact they have to be, the bound alone decides.
A program may use at most 128 MiB of HBM per device.

v0:
```python
import jax
import jax.numpy as jnp
from jax import lax
from jax.sharding import PartitionSpec as P

SWEEPS = 4
ITERS = 2
RELAX = 2.0 / 3.0


def padded(value, sides, width):
    for axis, dim in sides:
        count, length = (lax.axis_size(axis), value.shape[dim])
        up = [(i, (i + 1) % count) for i in range(count - 1)]
        down = [(j, i) for i, j in up]
        last = lax.slice_in_dim(value, length - width, length, axis=dim)
        leading = lax.slice_in_dim(value, 0, width, axis=dim)
        before = lax.ppermute(last, axis, up)
        after = lax.ppermute(leading, axis, down)
        value = jnp.concatenate([before, value, after], axis=dim)
    return value


def pad_cond(cond):
    return jnp.pad(cond, ((0, 0), (1, 1), (1, 1), (1, 1)))


def stencil(padded_free, padded_cond, field, storage, free):
    middle = padded_free[1:-1, 1:-1, 1:-1]
    total = storage * middle
    total = (
        total
        + padded_cond[0, 1:-1, 1:-1, 1:-1] * (middle - padded_free[2:, 1:-1, 1:-1])
        + padded_cond[0, :-2, 1:-1, 1:-1] * (middle - padded_free[:-2, 1:-1, 1:-1])
    )
    total = (
        total
        + padded_cond[1, 1:-1, 1:-1, 1:-1] * (middle - padded_free[1:-1, 2:, 1:-1])
        + padded_cond[1, 1:-1, :-2, 1:-1] * (middle - padded_free[1:-1, :-2, 1:-1])
    )
    total = (
        total
        + padded_cond[2, 1:-1, 1:-1, 1:-1] * (middle - padded_free[1:-1, 1:-1, 2:])
        + padded_cond[2, 1:-1, 1:-1, :-2] * (middle - padded_free[1:-1, 1:-1, :-2])
    )
    return free * total + (1.0 - free) * field


def diagonal_of(padded_cond, storage, free):
    total = storage + padded_cond[0, 1:-1, 1:-1, 1:-1] + padded_cond[0, :-2, 1:-1, 1:-1]
    total = total + padded_cond[1, 1:-1, 1:-1, 1:-1] + padded_cond[1, 1:-1, :-2, 1:-1]
    total = total + padded_cond[2, 1:-1, 1:-1, 1:-1] + padded_cond[2, 1:-1, 1:-1, :-2]
    return free * total + (1.0 - free)


def jacobi(rhs_box, padded_cond, diagonal, storage_box, free_box):
    guess = jnp.zeros_like(rhs_box)
    for sweep in range(SWEEPS):
        image = stencil(jnp.pad(free_box * guess, 1), padded_cond, guess, storage_box, free_box)
        guess = guess + RELAX * (rhs_box - image) / diagonal
    return guess


def project(basis, field):
    return jnp.dot(
        basis.reshape(basis.shape[0], -1), field.reshape(-1), precision=lax.Precision.HIGHEST
    )


def expand(basis, weights, field):
    return jnp.dot(
        weights, basis.reshape(basis.shape[0], -1), precision=lax.Precision.HIGHEST
    ).reshape(field.shape)


def gather_coarse(values):
    return lax.all_gather(values, ("gx", "gy", "gz"), axis=0, tiled=True)


def residual_rim(field):
    return padded(field, (("gx", 0), ("gy", 1), ("gz", 2)), 2)


def norm_sum(value):
    return lax.psum(value, ("gx", "gy", "gz"))


def shards(right_side, conductance, storage, dirichlet, basis, coarse_inverse):
    free = 1.0 - dirichlet.astype(jnp.float32)
    stacked = jnp.concatenate([conductance, storage[None], free[None]], axis=0)
    wide = padded(stacked, (("gx", 1), ("gy", 2), ("gz", 3)), 3)
    cond_face = wide[:3, 2:-2, 2:-2, 2:-2]
    free_face = wide[4, 2:-2, 2:-2, 2:-2]
    cond_box = wide[:3, 1:-1, 1:-1, 1:-1]
    storage_box = wide[3, 1:-1, 1:-1, 1:-1]
    free_box = wide[4, 1:-1, 1:-1, 1:-1]
    box_cond = pad_cond(cond_box)
    box_diag = diagonal_of(box_cond, storage_box, free_box)

    def schwarz(rhs_box):
        return jacobi(rhs_box, box_cond, box_diag, storage_box, free_box)[2:-2, 2:-2, 2:-2]

    solution = jnp.zeros_like(right_side)
    residual = right_side
    rhs_box = residual_rim(residual)
    coarse_now = project(basis, residual)
    weights = jnp.dot(coarse_inverse, gather_coarse(coarse_now), precision=lax.Precision.HIGHEST)
    precond = schwarz(rhs_box) + expand(basis, weights, residual)
    norm_now = norm_sum(jnp.sum(residual * precond))
    direction = precond
    for step in range(ITERS):
        near_dir = padded(direction, (("gx", 0), ("gy", 1), ("gz", 2)), 1)
        image = stencil(free_face * near_dir, cond_face, direction, storage, free)
        local_curve = jnp.sum(direction * image)
        curvature = lax.psum(local_curve, ("gx", "gy", "gz"))
        alpha = norm_now / curvature
        solution = solution + alpha * direction
        residual = residual - alpha * image
        if step + 1 < ITERS:
            rhs_box = residual_rim(residual)
            coarse_now = project(basis, residual)
            gathered = gather_coarse(coarse_now)
            weights = jnp.dot(coarse_inverse, gathered, precision=lax.Precision.HIGHEST)
            precond = schwarz(rhs_box) + expand(basis, weights, residual)
            norm_next = norm_sum(jnp.sum(residual * precond))
            direction = precond + norm_next / norm_now * direction
            norm_now = norm_next
    return (solution, residual)


def solution(mesh):
    placed = (
        P("gx", "gy", "gz"),
        P(None, "gx", "gy", "gz"),
        P("gx", "gy", "gz"),
        P("gx", "gy", "gz"),
        P(None, "gx", "gy", "gz"),
        P(("gx", "gy", "gz"), None),
    )
    return jax.shard_map(
        shards,
        mesh=mesh,
        in_specs=placed,
        out_specs=(P("gx", "gy", "gz"), P("gx", "gy", "gz")),
        check_vma=False,
    )
```

profile of v0, /device:TPU:1, one launch (start us, length us, event | category | flops | bytes accessed | tf_op | source)
XLA Modules:
  0.0 572.3 jit_solution(1241836847515531308)
XLA Ops:
  2.9 4.6 collective-permute-start.6
  10.3 3.6 collective-permute-start
  15.8 8.8 %fusion.8 = f32[16]{0:T(128)S(1)} fusion(f32[16,16,16,256]{3,2,1,0:T(8,128)} %param.10, f32[16,16,256,1]{2,1,0,3:T(8,128)} %bitcast.289), kind=kOutput, calls=%fused_computation.14 | convolution fusion | flops 12582912 | bytes 4456512 | tf_op jit(solution)/shard_map/dot_general | solution.py:65
  24.8 66.8 %all-reduce.8 = f32[2048]{0:T(1024)S(1)} all-reduce(f32[2048]{0:T(1024)S(1)} %dynamic-update-slice), channel_id=1, replica_groups=mesh['gx'=8,'gy'=4,'gz'=4] {'gx','gy','gz'}, use_global_device_ids=true, to_apply=%add.8 | all-reduce | flops 2048 | bytes 16384
  92.0 2.4 collective-permute-start.2
  98.7 4.7 collective-permute-start.8
  105.7 5.1 fusion.2
  110.9 8.1 %copy.37 = f32[5,22,16,256]{2,1,3,0:T(8,128)} copy(f32[5,22,16,256]{3,2,1,0:T(8,128)S(1)} %pad_maximum_fusion.2) | data formatting | bytes 3604480 | tf_op jit(solution)/shard_map/concatenate | solution.py:20
  119.0 9.0 %copy.36 = f32[5,22,3,256]{2,1,3,0:T(8,128)} copy(f32[5,22,3,256]{3,1,2,0:T(8,128)} %collective-permute-done.8) | data formatting | bytes 675840 | tf_op jit(solution)/shard_map/ppermute | solution.py:18
  128.0 9.0 %copy.38 = f32[5,22,3,256]{2,1,3,0:T(8,128)} copy(f32[5,22,3,256]{3,1,2,0:T(8,128)} %collective-permute-done.9) | data formatting | bytes 675840 | tf_op jit(solution)/shard_map/ppermute | solution.py:19
  137.0 16.9 %pad_maximum_fusion = f32[5,22,22,256]{2,1,3,0:T(8,128)S(1)} fusion(f32[5,22,3,256]{2,1,3,0:T(8,128)} %copy.38, f32[5,22,16,256]{2,1,3,0:T(8,128)} %copy.37, f32[5,22,3,256]{2,1,3,0:T(8,128)} %copy.36), kind=kLoop, calls=%fused_computation | loop fusion | flops 1239040 | bytes 4956160 | tf_op jit(solution)/shard_map/concatenate | solution.py:20
  153.8 5.4 copy-done.4
  160.0 2.7 collective-permute-start.10
  164.9 4.0 collective-permute-start.4
  170.4 9.2 %copy.40 = f32[5,22,22,256]{3,2,1,0:T(8,128)S(1)} copy(f32[5,22,22,256]{2,1,3,0:T(8,128)} %copy-done.4) | data formatting | bytes 4956160 | tf_op jit(solution)/shard_map/concatenate | solution.py:20
  179.6 3.1 copy.39
  184.6 3.2 pad_maximum_fusion.1
  191.2 3.7 fusion.213
  196.9 2.7 fusion.217
  201.5 2.1 fusion.208
  203.7 4.9 collective-permute-start.12
  208.6 2.3 collective-permute-start.13
  210.9 2.7 collective-permute-done.13
  213.7 4.3 collective-permute-start.14
  219.3 3.2 collective-permute-done.15
  222.7 4.3 collective-permute-start.16
  229.4 2.7 collective-permute-done.16
  232.2 3.9 collective-permute-done.17
  236.8 2.2 multiply_reduce_fusion.2
  239.0 63.0 %all-reduce.10 = (f32[]{:T(128)}, f32[]{:T(128)}) all-reduce(f32[]{:T(128)} %get-tuple-element.5, f32[]{:T(128)} %get-tuple-element.4), channel_id=1, replica_groups=mesh['gx'=8,'gy'=4,'gz'=4] {'gx','gy','gz'}, use_global_device_ids=true, to_apply=%region_1.2 | all-reduce | flops 2 | bytes 16 | tf_op jit(solution)/shard_map/psum | solution.py:85
  304.5 3.0 collective-permute-start.18
  309.4 8.6 %fusion.11 = f32[16]{0:T(128)S(1)} fusion(f32[16,16,16,256]{3,2,1,0:T(8,128)} %param.10, f32[16,16,256,1]{2,1,0,3:T(8,128)S(1)} %bitcast.285), kind=kOutput, calls=%fused_computation.15 | convolution fusion | flops 12582912 | bytes 4456512 | tf_op jit(solution)/shard_map/dot_general | solution.py:65
  318.3 63.0 %all-reduce.9 = f32[2048]{0:T(1024)S(1)} all-reduce(f32[2048]{0:T(1024)S(1)} %dynamic-update-slice.1), channel_id=1, replica_groups=mesh['gx'=8,'gy'=4,'gz'=4] {'gx','gy','gz'}, use_global_device_ids=true, to_apply=%add.9 | all-reduce | flops 2048 | bytes 16384
  381.4 2.7 collective-permute-start.20
  385.6 3.2 collective-permute-done.21
  392.3 6.4 %fusion = f32[1,16,16,256]{3,0,2,1:T(1,128)S(1)} fusion(f32[16,1,1,1]{0,1,3,2:T(1,128)S(1)} %convolution_bitcast_fusion, f32[16,16,256,16]{2,1,0,3:T(8,128)} %bitcast.283), kind=kOutput, calls=%fused_computation.2 | convolution fusion | flops 12582912 | bytes 4456512 | tf_op jit(solution)/shard_map/dot_general | solution.py:71
  399.5 2.0 fusion.216
  405.1 2.5 multiply_reduce_fusion.1
  407.6 67.1 %psum.30 = f32[]{:T(128)} all-reduce(f32[]{:T(128)} %get-tuple-element.10), channel_id=1, replica_groups=mesh['gx'=8,'gy'=4,'gz'=4] {'gx','gy','gz'}, use_global_device_ids=true, to_apply=%region_5.6 | all-reduce | flops 1 | bytes 8 | tf_op jit(solution)/shard_map/psum | solution.py:85
  476.9 2.3 collective-permute-start.24
  479.1 2.1 collective-permute-start.25
  481.2 3.0 collective-permute-done.25
  484.2 2.3 collective-permute-start.26
  488.0 3.2 collective-permute-done.27
  494.6 3.9 collective-permute-done.28
  498.5 3.9 collective-permute-done.29
  504.2 2.4 multiply_reduce_fusion
  506.7 63.2 %psum.31 = f32[]{:T(128)} all-reduce(f32[]{:T(128)} %get-tuple-element.8), channel_id=1, replica_groups=mesh['gx'=8,'gy'=4,'gz'=4] {'gx','gy','gz'}, use_global_device_ids=true, to_apply=%region_7.8 | all-reduce | flops 1 | bytes 8 | tf_op jit(solution)/shard_map/psum | solution.py:115
  (146 shorter events, 53.1 us)
Async XLA Ops:
  0.6 91.0 %copy-start = (f32[16,2048]{1,0:T(8,128)S(1)}, f32[16,2048]{1,0:T(8,128)}, u32[]{:S(2)}) copy-start(f32[16,2048]{1,0:T(8,128)} %param.11) | copy-start | bytes 393220
  0.6 95.8 %copy-start.15 = (f32[16,16,256]{2,1,0:T(8,128)S(1)}, f32[16,16,256]{2,1,0:T(8,128)}, u32[]{:S(2)}) copy-start(f32[16,16,256]{2,1,0:T(8,128)} %param.8) | copy-start | bytes 786436
  0.7 95.8 %copy-start.7 = (f32[3,16,16,256]{3,2,1,0:T(8,128)S(1)}, f32[3,16,16,256]{3,2,1,0:T(8,128)}, u32[]{:S(2)}) copy-start(f32[3,16,16,256]{3,2,1,0:T(8,128)} %param.7) | copy-start | bytes 2359300
  0.7 91.3 %copy-start.16 = (f32[16,16,256]{2,1,0:T(8,128)S(1)}, f32[16,16,256]{2,1,0:T(8,128)}, u32[]{:S(2)}) copy-start(f32[16,16,256]{2,1,0:T(8,128)} %param.6) | copy-start | bytes 786436
  1.8 95.9 %copy-start.18 = (f32[1,16,16,256]{3,2,1,0:T(8,128)}, f32[1,16,16,256]{3,2,1,0:T(8,128)S(1)}, u32[]{:S(2)}) copy-start(f32[1,16,16,256]{3,2,1,0:T(8,128)S(1)} %fusion.212) | copy-start | bytes 786436
  2.9 92.8 %collective-permute-start.6 = (f32[5,3,16,256]{3,2,1,0:T(8,128)S(1)}, f32[5,3,16,256]{3,2,1,0:T(8,128)S(1)}, u32[]{:S(2)}, u32[]{:S(2)}) collective-permute-start(f32[5,3,16,256]{3,2,1,0:T(8,128)S(1)} %get-tuple-element.36), channel_id=1, source_target_pairs={{0,16},{16,32},{32,48},{48,64},{64,80},{80,96},{96,112},{1,17},{17... | collective-permute-start | bytes 737288 | tf_op jit(solution)/shard_map/ppermute | solution.py:18
  7.6 88.9 %collective-permute-start.7 = (f32[5,3,16,256]{3,2,1,0:T(8,128)S(1)}, f32[5,3,16,256]{3,2,1,0:T(8,128)}, u32[]{:S(2)}, u32[]{:S(2)}) collective-permute-start(f32[5,3,16,256]{3,2,1,0:T(8,128)S(1)} %get-tuple-element.37), channel_id=1, source_target_pairs={{16,0},{32,16},{48,32},{64,48},{80,64},{96,80},{112,96},{17,1},{33... | collective-permute-start | bytes 737288 | tf_op jit(solution)/shard_map/ppermute | solution.py:19
  10.3 81.6 %collective-permute-start = (f32[2,16,256]{2,1,0:T(8,128)S(1)}, f32[2,16,256]{2,1,0:T(8,128)S(1)}, u32[]{:S(2)}, u32[]{:S(2)}) collective-permute-start(f32[2,16,256]{2,1,0:T(8,128)S(1)} %get-tuple-element.61), channel_id=1, source_target_pairs={{0,16},{16,32},{32,48},{48,64},{64,80},{80,96},{96,112},{1,17},{17... | collective-permute-start | bytes 98312 | tf_op jit(solution)/shard_map/ppermute | solution.py:18
  13.9 78.1 %collective-permute-start.1 = (f32[2,16,256]{2,1,0:T(8,128)S(1)}, f32[2,16,256]{2,1,0:T(8,128)S(1)}, u32[]{:S(2)}, u32[]{:S(2)}) collective-permute-start(f32[2,16,256]{2,1,0:T(8,128)S(1)} %get-tuple-element.60), channel_id=1, source_target_pairs={{16,0},{32,16},{48,32},{64,48},{80,64},{96,80},{112,96},{17,1},{33... | collective-permute-start | bytes 98312 | tf_op jit(solution)/shard_map/ppermute | solution.py:19
  92.0 18.8 %copy-start.22 = (f32[20,16,256]{2,1,0:T(8,128)}, f32[20,16,256]{2,1,0:T(8,128)S(1)}, u32[]{:S(2)}) copy-start(f32[20,16,256]{2,1,0:T(8,128)S(1)} %constant_dynamic-update-slice_fusion) | copy-start | bytes 983044
  92.0 18.7 %collective-permute-start.2 = (f32[20,2,256]{2,1,0:T(2,128)S(1)}, f32[20,2,256]{2,1,0:T(2,128)S(1)}, u32[]{:S(2)}, u32[]{:S(2)}) collective-permute-start(f32[20,2,256]{2,1,0:T(2,128)S(1)} %get-tuple-element.48), channel_id=1, source_target_pairs={{0,4},{4,8},{8,12},{1,5},{5,9},{9,13},{2,6},{6,10},{10,14},{3,7},{... | collective-permute-start | bytes 122888 | tf_op jit(solution)/shard_map/ppermute | solution.py:18
  94.5 16.3 %collective-permute-start.3 = (f32[20,2,256]{2,1,0:T(2,128)S(1)}, f32[20,2,256]{2,1,0:T(2,128)S(1)}, u32[]{:S(2)}, u32[]{:S(2)}) collective-permute-start(f32[20,2,256]{2,1,0:T(2,128)S(1)} %get-tuple-element.49), channel_id=1, source_target_pairs={{4,0},{8,4},{12,8},{5,1},{9,5},{13,9},{6,2},{10,6},{14,10},{7,3},{... | collective-permute-start | bytes 122888 | tf_op jit(solution)/shard_map/ppermute | solution.py:19
  98.7 20.3 %collective-permute-start.8 = (f32[5,22,3,256]{3,1,2,0:T(8,128)}, f32[5,22,3,256]{3,1,2,0:T(8,128)}, u32[]{:S(2)}, u32[]{:S(2)}) collective-permute-start(f32[5,22,3,256]{3,1,2,0:T(8,128)} %copy.55), channel_id=1, source_target_pairs={{0,4},{4,8},{8,12},{1,5},{5,9},{9,13},{2,6},{6,10},{10,14},{3,7},{... | collective-permute-start | bytes 1013768 | tf_op jit(solution)/shard_map/ppermute | solution.py:18
  104.3 23.8 %collective-permute-start.9 = (f32[5,22,3,256]{3,1,2,0:T(8,128)}, f32[5,22,3,256]{3,1,2,0:T(8,128)}, u32[]{:S(2)}, u32[]{:S(2)}) collective-permute-start(f32[5,22,3,256]{3,1,2,0:T(8,128)} %copy.56), channel_id=1, source_target_pairs={{4,0},{8,4},{12,8},{5,1},{9,5},{13,9},{6,2},{10,6},{14,10},{7,3},{... | collective-permute-start | bytes 1013768 | tf_op jit(solution)/shard_map/ppermute | solution.py:19
  160.0 19.6 %collective-permute-start.10 = (f32[5,22,22,3]{2,1,3,0:T(8,128)}, f32[5,22,22,3]{2,1,3,0:T(8,128)}, u32[]{:S(2)}, u32[]{:S(2)}) collective-permute-start(f32[5,22,22,3]{2,1,3,0:T(8,128)} %get-tuple-element.30), channel_id=1, source_target_pairs={{0,1},{1,2},{2,3},{4,5},{5,6},{6,7},{8,9},{9,10},{10,11},{12,13},{... | collective-permute-start | bytes 87128 | tf_op jit(solution)/shard_map/ppermute | solution.py:18
  162.7 20.0 %collective-permute-start.11 = (f32[5,22,22,3]{2,1,3,0:T(8,128)}, f32[5,22,22,3]{2,1,3,0:T(8,128)S(1)}, u32[]{:S(2)}, u32[]{:S(2)}) collective-permute-start(f32[5,22,22,3]{2,1,3,0:T(8,128)} %get-tuple-element.31), channel_id=1, source_target_pairs={{1,0},{2,1},{3,2},{5,4},{6,5},{7,6},{9,8},{10,9},{11,10},{13,12},{... | collective-permute-start | bytes 87128 | tf_op jit(solution)/shard_map/ppermute | solution.py:19
  164.9 25.7 %collective-permute-start.4 = (f32[20,20,2]{2,1,0:T(8,128)}, f32[20,20,2]{2,1,0:T(8,128)S(1)}, u32[]{:S(2)}, u32[]{:S(2)}) collective-permute-start(f32[20,20,2]{2,1,0:T(8,128)} %get-tuple-element.40), channel_id=1, source_target_pairs={{0,1},{1,2},{2,3},{4,5},{5,6},{6,7},{8,9},{9,10},{10,11},{12,13},{... | collective-permute-start | bytes 9608 | tf_op jit(solution)/shard_map/ppermute | solution.py:18
  168.9 22.4 %collective-permute-start.5 = (f32[20,20,2]{2,1,0:T(8,128)}, f32[20,20,2]{2,1,0:T(8,128)}, u32[]{:S(2)}, u32[]{:S(2)}) collective-permute-start(f32[20,20,2]{2,1,0:T(8,128)} %get-tuple-element.41), channel_id=1, source_target_pairs={{1,0},{2,1},{3,2},{5,4},{6,5},{7,6},{9,8},{10,9},{11,10},{13,12},{... | collective-permute-start | bytes 9608 | tf_op jit(solution)/shard_map/ppermute | solution.py:19
  187.8 48.3 %copy-start.1 = (f32[5,22,22,262]{3,2,1,0:T(8,128)}, f32[5,22,22,262]{3,2,1,0:T(8,128)S(1)}, u32[]{:S(2)}) copy-start(f32[5,22,22,262]{3,2,1,0:T(8,128)S(1)} %pad_maximum_fusion.1) | copy-start | bytes 7608484
  201.4 37.6 %copy-start.21 = (f32[20,20,260]{2,1,0:T(8,128)}, f32[20,20,260]{2,1,0:T(8,128)S(1)}, u32[]{:S(2)}) copy-start(f32[20,20,260]{2,1,0:T(8,128)S(1)} %get-tuple-element.32) | copy-start | bytes 1248004
  201.4 35.3 %copy-start.6 = (f32[5,22,22,256]{3,2,1,0:T(8,128)S(1)}, f32[5,22,22,256]{3,2,1,0:T(8,128)}, u32[]{:S(2)}) copy-start(f32[5,22,22,256]{3,2,1,0:T(8,128)} %copy-done.5) | copy-start | bytes 7434244
  201.4 35.3 %copy-start.8 = (f32[3,16,16,256]{3,2,1,0:T(8,128)S(1)}, f32[3,16,16,256]{3,2,1,0:T(8,128)}, u32[]{:S(2)}) copy-start(f32[3,16,16,256]{3,2,1,0:T(8,128)} %param.7) | copy-start | bytes 2359300
  201.4 35.3 %copy-start.12 = (f32[5,22,22,3]{3,2,1,0:T(8,128)S(1)}, f32[5,22,22,3]{3,2,1,0:T(8,128)}, u32[]{:S(2)}) copy-start(f32[5,22,22,3]{3,2,1,0:T(8,128)} %copy.39) | copy-start | bytes 87124
  201.5 35.3 %copy-start.17 = (f32[16,16,256]{2,1,0:T(8,128)S(1)}, f32[16,16,256]{2,1,0:T(8,128)}, u32[]{:S(2)}) copy-start(f32[16,16,256]{2,1,0:T(8,128)} %param.6) | copy-start | bytes 786436
  201.5 35.3 %copy-start.19 = (f32[1,16,16,256]{3,2,1,0:T(8,128)S(1)}, f32[1,16,16,256]{3,2,1,0:T(8,128)}, u32[]{:S(2)}) copy-start(f32[1,16,16,256]{3,2,1,0:T(8,128)} %copy-done.18) | copy-start | bytes 786436
  201.5 35.3 %copy-start.20 = (s32[16,16,256]{2,1,0:T(8,128)S(1)}, s32[16,16,256]{2,1,0:T(8,128)}, u32[]{:S(2)}) copy-start(s32[16,16,256]{2,1,0:T(8,128)} %param.9) | copy-start | bytes 786436
  201.5 35.3 %copy-start.26 = (f32[5,3,16,256]{3,2,1,0:T(8,128)S(1)}, f32[5,3,16,256]{3,2,1,0:T(8,128)}, u32[]{:S(2)}) copy-start(f32[5,3,16,256]{3,2,1,0:T(8,128)} %copy-done.25) | copy-start | bytes 737284
  203.7 35.4 %copy-start.10 = (f32[16,16,256]{2,1,0:T(8,128)}, f32[16,16,256]{2,1,0:T(8,128)S(1)}, u32[]{:S(2)}) copy-start(f32[16,16,256]{2,1,0:T(8,128)S(1)} %fusion.208) | copy-start | bytes 786436
  203.7 7.3 %collective-permute-start.12 = (f32[1,16,256]{2,1,0:T(8,128)S(1)}, f32[1,16,256]{2,1,0:T(8,128)S(1)}, u32[]{:S(2)}, u32[]{:S(2)}) collective-permute-start(f32[1,16,256]{2,1,0:T(8,128)S(1)} %get-tuple-element.58), channel_id=1, source_target_pairs={{0,16},{16,32},{32,48},{48,64},{64,80},{80,96},{96,112},{1,17},{17... | collective-permute-start | bytes 49160 | tf_op jit(solution)/shard_map/ppermute | solution.py:18
  208.6 5.1 collective-permute-start.13
  213.7 5.6 collective-permute-start.14
  218.0 4.5 collective-permute-start.15
  222.7 9.5 %collective-permute-start.16 = (f32[18,18,1]{2,1,0:T(8,128)S(1)}, f32[18,18,1]{2,1,0:T(8,128)S(1)}, u32[]{:S(2)}, u32[]{:S(2)}) collective-permute-start(f32[18,18,1]{2,1,0:T(8,128)S(1)} %get-tuple-element.44), channel_id=1, source_target_pairs={{0,1},{1,2},{2,3},{4,5},{5,6},{6,7},{8,9},{9,10},{10,11},{12,13},{... | collective-permute-start | bytes 3896 | tf_op jit(solution)/shard_map/ppermute | solution.py:18
  227.0 9.1 %collective-permute-start.17 = (f32[18,18,1]{2,1,0:T(8,128)S(1)}, f32[18,18,1]{2,1,0:T(8,128)S(1)}, u32[]{:S(2)}, u32[]{:S(2)}) collective-permute-start(f32[18,18,1]{2,1,0:T(8,128)S(1)} %get-tuple-element.45), channel_id=1, source_target_pairs={{1,0},{2,1},{3,2},{5,4},{6,5},{7,6},{9,8},{10,9},{11,10},{13,12},{... | collective-permute-start | bytes 3896 | tf_op jit(solution)/shard_map/ppermute | solution.py:19
  304.5 76.9 %collective-permute-start.18 = (f32[2,16,256]{2,1,0:T(8,128)S(1)}, f32[2,16,256]{2,1,0:T(8,128)S(1)}, u32[]{:S(2)}, u32[]{:S(2)}) collective-permute-start(f32[2,16,256]{2,1,0:T(8,128)S(1)} %get-tuple-element.56), channel_id=1, source_target_pairs={{0,16},{16,32},{32,48},{48,64},{64,80},{80,96},{96,112},{1,17},{17... | collective-permute-start | bytes 98312 | tf_op jit(solution)/shard_map/ppermute | solution.py:18
  307.5 73.8 %collective-permute-start.19 = (f32[2,16,256]{2,1,0:T(8,128)S(1)}, f32[2,16,256]{2,1,0:T(8,128)S(1)}, u32[]{:S(2)}, u32[]{:S(2)}) collective-permute-start(f32[2,16,256]{2,1,0:T(8,128)S(1)} %get-tuple-element.57), channel_id=1, source_target_pairs={{16,0},{32,16},{48,32},{64,48},{80,64},{96,80},{112,96},{17,1},{33... | collective-permute-start | bytes 98312 | tf_op jit(solution)/shard_map/ppermute | solution.py:19
  381.4 4.2 collective-permute-start.20
  384.1 4.7 collective-permute-start.21
  389.0 9.7 %collective-permute-start.22 = (f32[20,20,2]{2,1,0:T(8,128)S(1)}, f32[20,20,2]{2,1,0:T(8,128)S(1)}, u32[]{:S(2)}, u32[]{:S(2)}) collective-permute-start(f32[20,20,2]{2,1,0:T(8,128)S(1)} %get-tuple-element.38), channel_id=1, source_target_pairs={{0,1},{1,2},{2,3},{4,5},{5,6},{6,7},{8,9},{9,10},{10,11},{12,13},{... | collective-permute-start | bytes 9608 | tf_op jit(solution)/shard_map/ppermute | solution.py:18
  390.8 7.9 %collective-permute-start.23 = (f32[20,20,2]{2,1,0:T(8,128)S(1)}, f32[20,20,2]{2,1,0:T(8,128)S(1)}, u32[]{:S(2)}, u32[]{:S(2)}) collective-permute-start(f32[20,20,2]{2,1,0:T(8,128)S(1)} %get-tuple-element.39), channel_id=1, source_target_pairs={{1,0},{2,1},{3,2},{5,4},{6,5},{7,6},{9,8},{10,9},{11,10},{13,12},{... | collective-permute-start | bytes 9608 | tf_op jit(solution)/shard_map/ppermute | solution.py:19
  405.0 99.2 %copy-start.9 = (f32[3,16,16,256]{3,2,1,0:T(8,128)S(1)}, f32[3,16,16,256]{3,2,1,0:T(8,128)}, u32[]{:S(2)}) copy-start(f32[3,16,16,256]{3,2,1,0:T(8,128)} %param.7) | copy-start | bytes 2359300
  476.9 4.3 collective-permute-start.24
  479.1 5.1 collective-permute-start.25
  484.2 3.8 collective-permute-start.26
  486.6 84.6 %copy-start.11 = (f32[16,16,256]{2,1,0:T(8,128)S(1)}, f32[16,16,256]{2,1,0:T(8,128)}, u32[]{:S(2)}) copy-start(f32[16,16,256]{2,1,0:T(8,128)} %copy-done.10) | copy-start | bytes 786436
  486.6 4.6 collective-permute-start.27
  491.4 7.1 %collective-permute-start.28 = (f32[18,18,1]{2,1,0:T(8,128)S(1)}, f32[18,18,1]{2,1,0:T(8,128)S(1)}, u32[]{:S(2)}, u32[]{:S(2)}) collective-permute-start(f32[18,18,1]{2,1,0:T(8,128)S(1)} %get-tuple-element.42), channel_id=1, source_target_pairs={{0,1},{1,2},{2,3},{4,5},{5,6},{6,7},{8,9},{9,10},{10,11},{12,13},{... | collective-permute-start | bytes 3896 | tf_op jit(solution)/shard_map/ppermute | solution.py:18
  493.3 9.1 %collective-permute-start.29 = (f32[18,18,1]{2,1,0:T(8,128)S(1)}, f32[18,18,1]{2,1,0:T(8,128)S(1)}, u32[]{:S(2)}, u32[]{:S(2)}) collective-permute-start(f32[18,18,1]{2,1,0:T(8,128)S(1)} %get-tuple-element.43), channel_id=1, source_target_pairs={{1,0},{2,1},{3,2},{5,4},{6,5},{7,6},{9,8},{10,9},{11,10},{13,12},{... | collective-permute-start | bytes 3896 | tf_op jit(solution)/shard_map/ppermute | solution.py:19
  (14 other events, 94.5 us)
where the time goes:
time: 581 us; the launch traced here: 572 us
  blocking collectives  323 us (56%)
  starting transfers between devices  73.3 us (13%)
  local copies, waits for them, and re-layouts  55.9 us (10%)
  other arithmetic  55.2 us (10%)
  waiting for transfers between devices  29.9 us (5%)
  matrix products  29.2 us (5%)
    psum x2, blocking collectives, norm_sum(): return lax.psum(value, ('gx', 'gy', 'gz'))  130 us
    unnamed x2, blocking collectives  130 us
    psum x1, blocking collectives, shards(): curvature = lax.psum(local_curve, ('gx', 'gy', 'gz'))  63.2 us
    ppermute x15, starting transfers between devices, padded(): before = lax.ppermute(last, axis, up)  49.5 us
    ppermute x15, starting transfers between devices, padded(): after = lax.ppermute(leading, axis, down)  23.7 us
    ppermute x15, waiting for transfers between devices, padded(): after = lax.ppermute(leading, axis, down)  23.2 us
    concatenate x7, other arithmetic, padded(): value = jnp.concatenate([before, value, after], axis=dim)  21.5 us
    dot_general x2, matrix products, project(): jnp.dot(basis.reshape(basis.shape[0], -1), field.reshape(-1), precision=l...  17.4 us
  transfers between devices with their start and end apart: 30, of which 9 were waited for; matrix products, arithmetic and copies ran while one was open for 13% of the time, Pallas kernels for 0%

commit v1 on v0

--- a/solution.py
+++ b/solution.py
@@ -82,7 +82,7 @@
 
 
 def norm_sum(value):
-    return lax.psum(value, ("gx", "gy", "gz"))
+    return lax.psum(lax.psum(value, ("gy", "gz")), "gx")
 
 
 def shards(right_side, conductance, storage, dirichlet, basis, coarse_inverse):

time: 581 us -> 615 us (1.059)
  blocking collectives: 323 us -> 359 us
    psum x1 -> x2, blocking collectives: 63.2 us -> 124 us  [shards(): curvature = lax.psum(local_curve, ('gx', 'gy', 'gz'))]
    psum x2 -> x4, blocking collectives: 130 us -> 105 us  [norm_sum(): return lax.psum(lax.psum(value, ('gy', 'gz')), 'gx')]
  transfers between devices with their start and end apart: 30 -> 30, of which waited for: 9 -> 9; matrix products, arithmetic and copies ran while one was open for 13% -> 12% of each run, Pallas kernels for 0% -> 0%
where the time goes in v1:
time: 615 us; the launch traced here: 607 us
  blocking collectives  359 us (58%)
  starting transfers between devices  72.1 us (12%)
  local copies, waits for them, and re-layouts  56.2 us (9%)
  other arithmetic  55.1 us (9%)
  waiting for transfers between devices  29.4 us (5%)
  matrix products  29.2 us (5%)
    unnamed x2, blocking collectives  130 us
    psum x2, blocking collectives, shards(): curvature = lax.psum(local_curve, ('gx', 'gy', 'gz'))  124 us
    psum x4, blocking collectives, norm_sum(): return lax.psum(lax.psum(value, ('gy', 'gz')), 'gx')  105 us
    ppermute x15, starting transfers between devices, padded(): before = lax.ppermute(last, axis, up)  47.8 us
    ppermute x15, starting transfers between devices, padded(): after = lax.ppermute(leading, axis, down)  24.3 us
    ppermute x15, waiting for transfers between devices, padded(): after = lax.ppermute(leading, axis, down)  23 us
    concatenate x7, other arithmetic, padded(): value = jnp.concatenate([before, value, after], axis=dim)  21.5 us
    dot_general x2, matrix products, project(): jnp.dot(basis.reshape(basis.shape[0], -1), field.reshape(-1), precision=l...  17.4 us
  transfers between devices with their start and end apart: 30, of which 9 were waited for; matrix products, arithmetic and copies ran while one was open for 12% of the time, Pallas kernels for 0%

profile of v1, /device:TPU:1, one launch (start us, length us, event | category | flops | bytes accessed | tf_op | source)
XLA Modules:
  0.0 606.7 jit_solution(3490721301809254384)
XLA Ops:
  2.9 4.6 collective-permute-start.6
  10.3 3.6 collective-permute-start
  15.8 8.8 %fusion.8 = f32[16]{0:T(128)S(1)} fusion(f32[16,16,16,256]{3,2,1,0:T(8,128)} %param.10, f32[16,16,256,1]{2,1,0,3:T(8,128)} %bitcast.289), kind=kOutput, calls=%fused_computation.14 | convolution fusion | flops 12582912 | bytes 4456512 | tf_op jit(solution)/shard_map/dot_general | solution.py:65
  24.8 66.8 %all-reduce.8 = f32[2048]{0:T(1024)S(1)} all-reduce(f32[2048]{0:T(1024)S(1)} %dynamic-update-slice), channel_id=1, replica_groups=mesh['gx'=8,'gy'=4,'gz'=4] {'gx','gy','gz'}, use_global_device_ids=true, to_apply=%add.8 | all-reduce | flops 2048 | bytes 16384
  92.0 2.4 collective-permute-start.2
  98.7 4.7 collective-permute-start.8
  105.7 5.1 fusion.2
  110.9 8.1 %copy.37 = f32[5,22,16,256]{2,1,3,0:T(8,128)} copy(f32[5,22,16,256]{3,2,1,0:T(8,128)S(1)} %pad_maximum_fusion.2) | data formatting | bytes 3604480 | tf_op jit(solution)/shard_map/concatenate | solution.py:20
  119.0 9.1 %copy.36 = f32[5,22,3,256]{2,1,3,0:T(8,128)} copy(f32[5,22,3,256]{3,1,2,0:T(8,128)} %collective-permute-done.8) | data formatting | bytes 675840 | tf_op jit(solution)/shard_map/ppermute | solution.py:18
  128.2 9.0 %copy.38 = f32[5,22,3,256]{2,1,3,0:T(8,128)} copy(f32[5,22,3,256]{3,1,2,0:T(8,128)} %collective-permute-done.9) | data formatting | bytes 675840 | tf_op jit(solution)/shard_map/ppermute | solution.py:19
  137.2 16.9 %pad_maximum_fusion = f32[5,22,22,256]{2,1,3,0:T(8,128)S(1)} fusion(f32[5,22,3,256]{2,1,3,0:T(8,128)} %copy.38, f32[5,22,16,256]{2,1,3,0:T(8,128)} %copy.37, f32[5,22,3,256]{2,1,3,0:T(8,128)} %copy.36), kind=kLoop, calls=%fused_computation | loop fusion | flops 1239040 | bytes 4956160 | tf_op jit(solution)/shard_map/concatenate | solution.py:20
  154.0 5.4 copy-done.4
  160.2 2.7 collective-permute-start.10
  165.1 4.0 collective-permute-start.4
  170.6 9.2 %copy.40 = f32[5,22,22,256]{3,2,1,0:T(8,128)S(1)} copy(f32[5,22,22,256]{2,1,3,0:T(8,128)} %copy-done.4) | data formatting | bytes 4956160 | tf_op jit(solution)/shard_map/concatenate | solution.py:20
  179.9 3.1 copy.39
  184.9 3.2 pad_maximum_fusion.1
  191.5 3.7 fusion.213
  197.2 2.7 fusion.217
  201.8 2.1 fusion.208
  204.0 4.9 collective-permute-start.12
  208.9 2.3 collective-permute-start.13
  211.2 2.7 collective-permute-done.13
  214.0 4.3 collective-permute-start.14
  219.6 3.2 collective-permute-done.15
  223.0 4.3 collective-permute-start.16
  229.7 2.7 collective-permute-done.16
  232.5 3.9 collective-permute-done.17
  237.1 2.1 multiply_reduce_fusion.2
  239.3 29.8 %psum.42 = f32[]{:T(128)} all-reduce(f32[]{:T(128)} %get-tuple-element.5), channel_id=1, replica_groups=mesh['gx'=8,'gy'=4,'gz'=4] {'gy','gz'}, use_global_device_ids=true, to_apply=%region_1.2 | all-reduce | flops 1 | bytes 8 | tf_op jit(solution)/shard_map/psum | solution.py:85
  269.1 20.0 %psum.43 = f32[]{:T(128)} all-reduce(f32[]{:T(128)} %psum.42), channel_id=1, replica_groups=mesh['gx'=8,'gy'=4,'gz'=4] {'gx'}, use_global_device_ids=true, to_apply=%region_2.3 | all-reduce | flops 1 | bytes 8 | tf_op jit(solution)/shard_map/psum | solution.py:85
  289.1 62.4 %psum.44 = f32[]{:T(128)} all-reduce(f32[]{:T(128)} %get-tuple-element.4), channel_id=1, replica_groups=mesh['gx'=8,'gy'=4,'gz'=4] {'gx','gy','gz'}, use_global_device_ids=true, to_apply=%region_4.5 | all-reduce | flops 1 | bytes 8 | tf_op jit(solution)/shard_map/psum | solution.py:115
  353.9 3.3 collective-permute-start.18
  359.2 8.6 %fusion.11 = f32[16]{0:T(128)S(1)} fusion(f32[16,16,16,256]{3,2,1,0:T(8,128)} %param.10, f32[16,16,256,1]{2,1,0,3:T(8,128)S(1)} %bitcast.285), kind=kOutput, calls=%fused_computation.15 | convolution fusion | flops 12582912 | bytes 4456512 | tf_op jit(solution)/shard_map/dot_general | solution.py:65
  368.0 63.1 %all-reduce.9 = f32[2048]{0:T(1024)S(1)} all-reduce(f32[2048]{0:T(1024)S(1)} %dynamic-update-slice.1), channel_id=1, replica_groups=mesh['gx'=8,'gy'=4,'gz'=4] {'gx','gy','gz'}, use_global_device_ids=true, to_apply=%add.9 | all-reduce | flops 2048 | bytes 16384
  431.1 2.6 collective-permute-start.20
  435.2 3.2 collective-permute-done.21
  442.1 6.4 %fusion = f32[1,16,16,256]{3,0,2,1:T(1,128)S(1)} fusion(f32[16,1,1,1]{0,1,3,2:T(1,128)S(1)} %convolution_bitcast_fusion, f32[16,16,256,16]{2,1,0,3:T(8,128)} %bitcast.283), kind=kOutput, calls=%fused_computation.2 | convolution fusion | flops 12582912 | bytes 4456512 | tf_op jit(solution)/shard_map/dot_general | solution.py:71
  454.9 2.5 multiply_reduce_fusion.1
  457.4 33.2 %psum.45 = f32[]{:T(128)} all-reduce(f32[]{:T(128)} %get-tuple-element.8), channel_id=1, replica_groups=mesh['gx'=8,'gy'=4,'gz'=4] {'gy','gz'}, use_global_device_ids=true, to_apply=%region_6.7 | all-reduce | flops 1 | bytes 8 | tf_op jit(solution)/shard_map/psum | solution.py:85
  490.6 21.6 %psum.46 = f32[]{:T(128)} all-reduce(f32[]{:T(128)} %psum.45), channel_id=1, replica_groups=mesh['gx'=8,'gy'=4,'gz'=4] {'gx'}, use_global_device_ids=true, to_apply=%region_7.8 | all-reduce | flops 1 | bytes 8 | tf_op jit(solution)/shard_map/psum | solution.py:85
  516.5 2.4 collective-permute-start.25
  518.9 2.6 collective-permute-done.25
  524.3 3.2 collective-permute-done.27
  530.5 3.6 collective-permute-done.28
  534.1 4.1 collective-permute-done.29
  540.0 2.4 multiply_reduce_fusion
  542.4 61.9 %psum.47 = f32[]{:T(128)} all-reduce(f32[]{:T(128)} %get-tuple-element.6), channel_id=1, replica_groups=mesh['gx'=8,'gy'=4,'gz'=4] {'gx','gy','gz'}, use_global_device_ids=true, to_apply=%region_9.10 | all-reduce | flops 1 | bytes 8 | tf_op jit(solution)/shard_map/psum | solution.py:115
  (149 shorter events, 58.1 us)
Async XLA Ops:
  0.6 91.0 %copy-start = (f32[16,2048]{1,0:T(8,128)S(1)}, f32[16,2048]{1,0:T(8,128)}, u32[]{:S(2)}) copy-start(f32[16,2048]{1,0:T(8,128)} %param.11) | copy-start | bytes 393220
  0.6 95.9 %copy-start.15 = (f32[16,16,256]{2,1,0:T(8,128)S(1)}, f32[16,16,256]{2,1,0:T(8,128)}, u32[]{:S(2)}) copy-start(f32[16,16,256]{2,1,0:T(8,128)} %param.8) | copy-start | bytes 786436
  0.7 95.8 %copy-start.7 = (f32[3,16,16,256]{3,2,1,0:T(8,128)S(1)}, f32[3,16,16,256]{3,2,1,0:T(8,128)}, u32[]{:S(2)}) copy-start(f32[3,16,16,256]{3,2,1,0:T(8,128)} %param.7) | copy-start | bytes 2359300
  0.7 91.3 %copy-start.16 = (f32[16,16,256]{2,1,0:T(8,128)S(1)}, f32[16,16,256]{2,1,0:T(8,128)}, u32[]{:S(2)}) copy-start(f32[16,16,256]{2,1,0:T(8,128)} %param.6) | copy-start | bytes 786436
  1.8 96.0 %copy-start.18 = (f32[1,16,16,256]{3,2,1,0:T(8,128)}, f32[1,16,16,256]{3,2,1,0:T(8,128)S(1)}, u32[]{:S(2)}) copy-start(f32[1,16,16,256]{3,2,1,0:T(8,128)S(1)} %fusion.212) | copy-start | bytes 786436
  2.9 92.8 %collective-permute-start.6 = (f32[5,3,16,256]{3,2,1,0:T(8,128)S(1)}, f32[5,3,16,256]{3,2,1,0:T(8,128)S(1)}, u32[]{:S(2)}, u32[]{:S(2)}) collective-permute-start(f32[5,3,16,256]{3,2,1,0:T(8,128)S(1)} %get-tuple-element.34), channel_id=1, source_target_pairs={{0,16},{16,32},{32,48},{48,64},{64,80},{80,96},{96,112},{1,17},{17... | collective-permute-start | bytes 737288 | tf_op jit(solution)/shard_map/ppermute | solution.py:18
  7.6 88.9 %collective-permute-start.7 = (f32[5,3,16,256]{3,2,1,0:T(8,128)S(1)}, f32[5,3,16,256]{3,2,1,0:T(8,128)}, u32[]{:S(2)}, u32[]{:S(2)}) collective-permute-start(f32[5,3,16,256]{3,2,1,0:T(8,128)S(1)} %get-tuple-element.35), channel_id=1, source_target_pairs={{16,0},{32,16},{48,32},{64,48},{80,64},{96,80},{112,96},{17,1},{33... | collective-permute-start | bytes 737288 | tf_op jit(solution)/shard_map/ppermute | solution.py:19
  10.3 81.6 %collective-permute-start = (f32[2,16,256]{2,1,0:T(8,128)S(1)}, f32[2,16,256]{2,1,0:T(8,128)S(1)}, u32[]{:S(2)}, u32[]{:S(2)}) collective-permute-start(f32[2,16,256]{2,1,0:T(8,128)S(1)} %get-tuple-element.59), channel_id=1, source_target_pairs={{0,16},{16,32},{32,48},{48,64},{64,80},{80,96},{96,112},{1,17},{17... | collective-permute-start | bytes 98312 | tf_op jit(solution)/shard_map/ppermute | solution.py:18
  13.9 78.1 %collective-permute-start.1 = (f32[2,16,256]{2,1,0:T(8,128)S(1)}, f32[2,16,256]{2,1,0:T(8,128)S(1)}, u32[]{:S(2)}, u32[]{:S(2)}) collective-permute-start(f32[2,16,256]{2,1,0:T(8,128)S(1)} %get-tuple-element.58), channel_id=1, source_target_pairs={{16,0},{32,16},{48,32},{64,48},{80,64},{96,80},{112,96},{17,1},{33... | collective-permute-start | bytes 98312 | tf_op jit(solution)/shard_map/ppermute | solution.py:19
  92.0 18.8 %copy-start.22 = (f32[20,16,256]{2,1,0:T(8,128)}, f32[20,16,256]{2,1,0:T(8,128)S(1)}, u32[]{:S(2)}) copy-start(f32[20,16,256]{2,1,0:T(8,128)S(1)} %constant_dynamic-update-slice_fusion) | copy-start | bytes 983044
  92.0 18.7 %collective-permute-start.2 = (f32[20,2,256]{2,1,0:T(2,128)S(1)}, f32[20,2,256]{2,1,0:T(2,128)S(1)}, u32[]{:S(2)}, u32[]{:S(2)}) collective-permute-start(f32[20,2,256]{2,1,0:T(2,128)S(1)} %get-tuple-element.46), channel_id=1, source_target_pairs={{0,4},{4,8},{8,12},{1,5},{5,9},{9,13},{2,6},{6,10},{10,14},{3,7},{... | collective-permute-start | bytes 122888 | tf_op jit(solution)/shard_map/ppermute | solution.py:18
  94.5 16.3 %collective-permute-start.3 = (f32[20,2,256]{2,1,0:T(2,128)S(1)}, f32[20,2,256]{2,1,0:T(2,128)S(1)}, u32[]{:S(2)}, u32[]{:S(2)}) collective-permute-start(f32[20,2,256]{2,1,0:T(2,128)S(1)} %get-tuple-element.47), channel_id=1, source_target_pairs={{4,0},{8,4},{12,8},{5,1},{9,5},{13,9},{6,2},{10,6},{14,10},{7,3},{... | collective-permute-start | bytes 122888 | tf_op jit(solution)/shard_map/ppermute | solution.py:19
  98.7 20.3 %collective-permute-start.8 = (f32[5,22,3,256]{3,1,2,0:T(8,128)}, f32[5,22,3,256]{3,1,2,0:T(8,128)}, u32[]{:S(2)}, u32[]{:S(2)}) collective-permute-start(f32[5,22,3,256]{3,1,2,0:T(8,128)} %copy.55), channel_id=1, source_target_pairs={{0,4},{4,8},{8,12},{1,5},{5,9},{9,13},{2,6},{6,10},{10,14},{3,7},{... | collective-permute-start | bytes 1013768 | tf_op jit(solution)/shard_map/ppermute | solution.py:18
  104.2 23.9 %collective-permute-start.9 = (f32[5,22,3,256]{3,1,2,0:T(8,128)}, f32[5,22,3,256]{3,1,2,0:T(8,128)}, u32[]{:S(2)}, u32[]{:S(2)}) collective-permute-start(f32[5,22,3,256]{3,1,2,0:T(8,128)} %copy.56), channel_id=1, source_target_pairs={{4,0},{8,4},{12,8},{5,1},{9,5},{13,9},{6,2},{10,6},{14,10},{7,3},{... | collective-permute-start | bytes 1013768 | tf_op jit(solution)/shard_map/ppermute | solution.py:19
  160.2 19.6 %collective-permute-start.10 = (f32[5,22,22,3]{2,1,3,0:T(8,128)}, f32[5,22,22,3]{2,1,3,0:T(8,128)}, u32[]{:S(2)}, u32[]{:S(2)}) collective-permute-start(f32[5,22,22,3]{2,1,3,0:T(8,128)} %get-tuple-element.28), channel_id=1, source_target_pairs={{0,1},{1,2},{2,3},{4,5},{5,6},{6,7},{8,9},{9,10},{10,11},{12,13},{... | collective-permute-start | bytes 87128 | tf_op jit(solution)/shard_map/ppermute | solution.py:18
  162.9 20.0 %collective-permute-start.11 = (f32[5,22,22,3]{2,1,3,0:T(8,128)}, f32[5,22,22,3]{2,1,3,0:T(8,128)S(1)}, u32[]{:S(2)}, u32[]{:S(2)}) collective-permute-start(f32[5,22,22,3]{2,1,3,0:T(8,128)} %get-tuple-element.29), channel_id=1, source_target_pairs={{1,0},{2,1},{3,2},{5,4},{6,5},{7,6},{9,8},{10,9},{11,10},{13,12},{... | collective-permute-start | bytes 87128 | tf_op jit(solution)/shard_map/ppermute | solution.py:19
  165.1 25.7 %collective-permute-start.4 = (f32[20,20,2]{2,1,0:T(8,128)}, f32[20,20,2]{2,1,0:T(8,128)S(1)}, u32[]{:S(2)}, u32[]{:S(2)}) collective-permute-start(f32[20,20,2]{2,1,0:T(8,128)} %get-tuple-element.38), channel_id=1, source_target_pairs={{0,1},{1,2},{2,3},{4,5},{5,6},{6,7},{8,9},{9,10},{10,11},{12,13},{... | collective-permute-start | bytes 9608 | tf_op jit(solution)/shard_map/ppermute | solution.py:18
  169.1 22.4 %collective-permute-start.5 = (f32[20,20,2]{2,1,0:T(8,128)}, f32[20,20,2]{2,1,0:T(8,128)}, u32[]{:S(2)}, u32[]{:S(2)}) collective-permute-start(f32[20,20,2]{2,1,0:T(8,128)} %get-tuple-element.39), channel_id=1, source_target_pairs={{1,0},{2,1},{3,2},{5,4},{6,5},{7,6},{9,8},{10,9},{11,10},{13,12},{... | collective-permute-start | bytes 9608 | tf_op jit(solution)/shard_map/ppermute | solution.py:19
  188.1 48.3 %copy-start.1 = (f32[5,22,22,262]{3,2,1,0:T(8,128)}, f32[5,22,22,262]{3,2,1,0:T(8,128)S(1)}, u32[]{:S(2)}) copy-start(f32[5,22,22,262]{3,2,1,0:T(8,128)S(1)} %pad_maximum_fusion.1) | copy-start | bytes 7608484
  201.7 37.6 %copy-start.21 = (f32[20,20,260]{2,1,0:T(8,128)}, f32[20,20,260]{2,1,0:T(8,128)S(1)}, u32[]{:S(2)}) copy-start(f32[20,20,260]{2,1,0:T(8,128)S(1)} %get-tuple-element.30) | copy-start | bytes 1248004
  201.7 35.3 %copy-start.6 = (f32[5,22,22,256]{3,2,1,0:T(8,128)S(1)}, f32[5,22,22,256]{3,2,1,0:T(8,128)}, u32[]{:S(2)}) copy-start(f32[5,22,22,256]{3,2,1,0:T(8,128)} %copy-done.5) | copy-start | bytes 7434244
  201.7 35.3 %copy-start.8 = (f32[3,16,16,256]{3,2,1,0:T(8,128)S(1)}, f32[3,16,16,256]{3,2,1,0:T(8,128)}, u32[]{:S(2)}) copy-start(f32[3,16,16,256]{3,2,1,0:T(8,128)} %param.7) | copy-start | bytes 2359300
  201.7 35.3 %copy-start.12 = (f32[5,22,22,3]{3,2,1,0:T(8,128)S(1)}, f32[5,22,22,3]{3,2,1,0:T(8,128)}, u32[]{:S(2)}) copy-start(f32[5,22,22,3]{3,2,1,0:T(8,128)} %copy.39) | copy-start | bytes 87124
  201.7 35.3 %copy-start.17 = (f32[16,16,256]{2,1,0:T(8,128)S(1)}, f32[16,16,256]{2,1,0:T(8,128)}, u32[]{:S(2)}) copy-start(f32[16,16,256]{2,1,0:T(8,128)} %param.6) | copy-start | bytes 786436
  201.8 35.3 %copy-start.19 = (f32[1,16,16,256]{3,2,1,0:T(8,128)S(1)}, f32[1,16,16,256]{3,2,1,0:T(8,128)}, u32[]{:S(2)}) copy-start(f32[1,16,16,256]{3,2,1,0:T(8,128)} %copy-done.18) | copy-start | bytes 786436
  201.8 35.3 %copy-start.20 = (s32[16,16,256]{2,1,0:T(8,128)S(1)}, s32[16,16,256]{2,1,0:T(8,128)}, u32[]{:S(2)}) copy-start(s32[16,16,256]{2,1,0:T(8,128)} %param.9) | copy-start | bytes 786436
  201.8 35.3 %copy-start.26 = (f32[5,3,16,256]{3,2,1,0:T(8,128)S(1)}, f32[5,3,16,256]{3,2,1,0:T(8,128)}, u32[]{:S(2)}) copy-start(f32[5,3,16,256]{3,2,1,0:T(8,128)} %copy-done.25) | copy-start | bytes 737284
  203.9 35.3 %copy-start.10 = (f32[16,16,256]{2,1,0:T(8,128)}, f32[16,16,256]{2,1,0:T(8,128)S(1)}, u32[]{:S(2)}) copy-start(f32[16,16,256]{2,1,0:T(8,128)S(1)} %fusion.208) | copy-start | bytes 786436
  204.0 7.3 %collective-permute-start.12 = (f32[1,16,256]{2,1,0:T(8,128)S(1)}, f32[1,16,256]{2,1,0:T(8,128)S(1)}, u32[]{:S(2)}, u32[]{:S(2)}) collective-permute-start(f32[1,16,256]{2,1,0:T(8,128)S(1)} %get-tuple-element.56), channel_id=1, source_target_pairs={{0,16},{16,32},{32,48},{48,64},{64,80},{80,96},{96,112},{1,17},{17... | collective-permute-start | bytes 49160 | tf_op jit(solution)/shard_map/ppermute | solution.py:18
  208.9 5.1 collective-permute-start.13
  214.0 5.6 collective-permute-start.14
  218.3 4.5 collective-permute-start.15
  223.0 9.5 %collective-permute-start.16 = (f32[18,18,1]{2,1,0:T(8,128)S(1)}, f32[18,18,1]{2,1,0:T(8,128)S(1)}, u32[]{:S(2)}, u32[]{:S(2)}) collective-permute-start(f32[18,18,1]{2,1,0:T(8,128)S(1)} %get-tuple-element.42), channel_id=1, source_target_pairs={{0,1},{1,2},{2,3},{4,5},{5,6},{6,7},{8,9},{9,10},{10,11},{12,13},{... | collective-permute-start | bytes 3896 | tf_op jit(solution)/shard_map/ppermute | solution.py:18
  227.2 9.1 %collective-permute-start.17 = (f32[18,18,1]{2,1,0:T(8,128)S(1)}, f32[18,18,1]{2,1,0:T(8,128)S(1)}, u32[]{:S(2)}, u32[]{:S(2)}) collective-permute-start(f32[18,18,1]{2,1,0:T(8,128)S(1)} %get-tuple-element.43), channel_id=1, source_target_pairs={{1,0},{2,1},{3,2},{5,4},{6,5},{7,6},{9,8},{10,9},{11,10},{13,12},{... | collective-permute-start | bytes 3896 | tf_op jit(solution)/shard_map/ppermute | solution.py:19
  353.9 77.2 %collective-permute-start.18 = (f32[2,16,256]{2,1,0:T(8,128)S(1)}, f32[2,16,256]{2,1,0:T(8,128)S(1)}, u32[]{:S(2)}, u32[]{:S(2)}) collective-permute-start(f32[2,16,256]{2,1,0:T(8,128)S(1)} %get-tuple-element.54), channel_id=1, source_target_pairs={{0,16},{16,32},{32,48},{48,64},{64,80},{80,96},{96,112},{1,17},{17... | collective-permute-start | bytes 98312 | tf_op jit(solution)/shard_map/ppermute | solution.py:18
  357.2 73.9 %collective-permute-start.19 = (f32[2,16,256]{2,1,0:T(8,128)S(1)}, f32[2,16,256]{2,1,0:T(8,128)S(1)}, u32[]{:S(2)}, u32[]{:S(2)}) collective-permute-start(f32[2,16,256]{2,1,0:T(8,128)S(1)} %get-tuple-element.55), channel_id=1, source_target_pairs={{16,0},{32,16},{48,32},{64,48},{80,64},{96,80},{112,96},{17,1},{33... | collective-permute-start | bytes 98312 | tf_op jit(solution)/shard_map/ppermute | solution.py:19
  431.1 4.1 collective-permute-start.20
  433.7 4.7 collective-permute-start.21
  438.7 9.8 %collective-permute-start.22 = (f32[20,20,2]{2,1,0:T(8,128)S(1)}, f32[20,20,2]{2,1,0:T(8,128)S(1)}, u32[]{:S(2)}, u32[]{:S(2)}) collective-permute-start(f32[20,20,2]{2,1,0:T(8,128)S(1)} %get-tuple-element.36), channel_id=1, source_target_pairs={{0,1},{1,2},{2,3},{4,5},{5,6},{6,7},{8,9},{9,10},{10,11},{12,13},{... | collective-permute-start | bytes 9608 | tf_op jit(solution)/shard_map/ppermute | solution.py:18
  440.6 7.9 %collective-permute-start.23 = (f32[20,20,2]{2,1,0:T(8,128)S(1)}, f32[20,20,2]{2,1,0:T(8,128)S(1)}, u32[]{:S(2)}, u32[]{:S(2)}) collective-permute-start(f32[20,20,2]{2,1,0:T(8,128)S(1)} %get-tuple-element.37), channel_id=1, source_target_pairs={{1,0},{2,1},{3,2},{5,4},{6,5},{7,6},{9,8},{10,9},{11,10},{13,12},{... | collective-permute-start | bytes 9608 | tf_op jit(solution)/shard_map/ppermute | solution.py:19
  454.8 85.1 %copy-start.9 = (f32[3,16,16,256]{3,2,1,0:T(8,128)S(1)}, f32[3,16,16,256]{3,2,1,0:T(8,128)}, u32[]{:S(2)}) copy-start(f32[3,16,16,256]{3,2,1,0:T(8,128)} %param.7) | copy-start | bytes 2359300
  514.5 4.3 collective-permute-start.24
  516.5 5.1 collective-permute-start.25
  521.5 2.7 collective-permute-start.26
  522.8 82.8 %copy-start.11 = (f32[16,16,256]{2,1,0:T(8,128)S(1)}, f32[16,16,256]{2,1,0:T(8,128)}, u32[]{:S(2)}) copy-start(f32[16,16,256]{2,1,0:T(8,128)} %copy-done.10) | copy-start | bytes 786436
  522.9 4.6 collective-permute-start.27
  527.7 6.4 %collective-permute-start.28 = (f32[18,18,1]{2,1,0:T(8,128)S(1)}, f32[18,18,1]{2,1,0:T(8,128)S(1)}, u32[]{:S(2)}, u32[]{:S(2)}) collective-permute-start(f32[18,18,1]{2,1,0:T(8,128)S(1)} %get-tuple-element.40), channel_id=1, source_target_pairs={{0,1},{1,2},{2,3},{4,5},{5,6},{6,7},{8,9},{9,10},{10,11},{12,13},{... | collective-permute-start | bytes 3896 | tf_op jit(solution)/shard_map/ppermute | solution.py:18
  529.0 9.2 %collective-permute-start.29 = (f32[18,18,1]{2,1,0:T(8,128)S(1)}, f32[18,18,1]{2,1,0:T(8,128)S(1)}, u32[]{:S(2)}, u32[]{:S(2)}) collective-permute-start(f32[18,18,1]{2,1,0:T(8,128)S(1)} %get-tuple-element.41), channel_id=1, source_target_pairs={{1,0},{2,1},{3,2},{5,4},{6,5},{7,6},{9,8},{10,9},{11,10},{13,12},{... | collective-permute-start | bytes 3896 | tf_op jit(solution)/shard_map/ppermute | solution.py:19
  (14 other events, 94.6 us)
